TPU v7x, 32 devices: a whole 2x2x4 slice. The times are simulated.
32 devices in a mesh: groups: 2 (over y), markov: 4 (over z), storage: 2 (over x), sub: 2 (over core).
Axes of the slice: x: 2, y: 2, z: 4, core: 2. Of those that a mesh axis runs over, the one named last changes fastest.
Arguments:
- expected_cot: bfloat16 [8192, 2048], P(('groups', 'markov'), ('storage', 'sub')), parts along dimension 0, may hold values from -192 to 192
- value_next: bfloat16 [8192, 2048], P(('groups', 'markov'), ('storage', 'sub')), parts along dimension 0, may hold values from -0.0024414062 to 0.0024414062
- transition: bfloat16 [8192, 4096], P(('groups', 'storage', 'sub'), 'markov'), parts along dimension 0, may hold values from 6.1035156e-05 to 0.0009765625
- section: int32 [2], P('groups'), parts along dimension 0, may hold values from 0 to 51
Outputs:
- section_adjoint: float32 [8192, 2048], P(('groups', 'markov'), ('storage', 'sub')), parts along dimension 0
- transition_grad: float32 [8192, 4096], P(('groups', 'storage', 'sub'), 'markov'), parts along dimension 0
There are 2 independent parts, one for each index of `groups`. A program takes and returns all parts, laid end to end along the dimension named above; each array names one. Nothing has to cross between parts.
All inputs are finite; a program needn't handle non-finite values.
Results may differ from a plain program's by a relative error of at most 0.0003.
Values may be sent and summed in bfloat16 or wider, within the bound.
A program may use at most 64 MiB of HBM per device.

v0:
```python
import jax
import jax.numpy as jnp
from jax import lax
from jax.sharding import PartitionSpec as P

discount_rate = 0.97


def shards(expected_cot, value_next, transition, section):
    discount_factor = jnp.exp(section[0].astype(jnp.float32) * jnp.log(jnp.float32(discount_rate)))
    cotangent_all = lax.all_gather(expected_cot, "markov", axis=0, tiled=True)
    adjoint_sum = lax.dot_general(
        lax.all_gather(transition, ("storage", "sub"), axis=0, tiled=True),
        cotangent_all,
        (((0,), (0,)), ((), ())),
        preferred_element_type=jnp.float32,
    )
    own_states = lax.all_to_all(
        cotangent_all, ("storage", "sub"), split_axis=0, concat_axis=1, tiled=True
    )
    gathered_values = lax.all_gather(value_next, ("storage", "sub"), axis=1, tiled=True)
    gradient_sum = lax.dot_general(
        own_states, gathered_values, (((1,), (1,)), ((), ())), preferred_element_type=jnp.float32
    )
    return (discount_factor * adjoint_sum, discount_factor * gradient_sum)


def solution(mesh):
    return jax.shard_map(
        shards,
        mesh=mesh,
        in_specs=(
            P(("groups", "markov"), ("storage", "sub")),
            P(("groups", "markov"), ("storage", "sub")),
            P(("groups", "storage", "sub"), "markov"),
            P("groups"),
        ),
        out_specs=(
            P(("groups", "markov"), ("storage", "sub")),
            P(("groups", "storage", "sub"), "markov"),
        ),
        check_vma=False,
    )
```

profile of v0, /device:TPU:0, one launch (start us, length us, event | category | flops | bytes accessed | tf_op | source)
XLA Modules:
  0.0 232.1 jit_solution(16197326605313307399)
XLA Ops:
  7.2 0.0 all-gather.6.cloned.1.call-start
  7.2 0.7 all-gather.6.cloned.1.call-update
  7.9 0.0 all-gather.8.cloned.1.call-start
  7.9 0.7 all-gather.8.cloned.1.call-update
  8.6 0.0 all-gather.4.cloned.1.call-start
  8.7 0.7 all-gather.4.cloned.1.call-update
  9.4 83.7 %all-gather.6.cloned.1.call-done = bf16[4096,512]{1,0:T(8,128)(2,1)} async-done(((bf16[1024,512]{1,0:T(8,128)(2,1)}), bf16[4096,512]{1,0:T(8,128)(2,1)}) %all-gather.6.cloned.1.call-update) | async-done | bytes 4194320 | tf_op jit(solution)/shard_map/all_gather | solution.py:11
  93.0 4.9 %all-to-all-start = ((bf16[4,1024,512]{2,1,0:T(8,128)(2,1)}), bf16[4,1024,512]{2,1,0:T(8,128)(2,1)}, u32[]{:S(2)}, u32[]{:S(2)}) async-start(bf16[4,1024,512]{2,1,0:T(8,128)(2,1)} %bitcast.8), calls=%async_computation | async-start | bytes 8388608 | tf_op jit(solution)/shard_map/all_to_all | solution.py:18
  98.6 75.7 %all-to-all-done = bf16[4,1024,512]{2,1,0:T(8,128)(2,1)} async-done(((bf16[4,1024,512]{2,1,0:T(8,128)(2,1)}), bf16[4,1024,512]{2,1,0:T(8,128)(2,1)}, u32[]{:S(2)}, u32[]{:S(2)}) %all-to-all-start) | async-done | bytes 4194336 | tf_op jit(solution)/shard_map/all_to_all | solution.py:18
  174.3 6.3 %copy.6 = bf16[1024,4,512]{0,2,1:T(8,128)(2,1)} copy(bf16[1024,4,512]{2,0,1:T(8,128)(2,1)} %bitcast.2) | data formatting | bytes 8388608 | tf_op jit(solution)/shard_map/all_to_all | solution.py:18
  180.6 0.0 all-gather.8.cloned.1.call-done
  180.6 10.0 %convolution_multiply_fusion = f32[1024,1024]{1,0:T(8,128)} fusion(bf16[1024,2048]{0,1:T(8,128)(2,1)} %bitcast.9, bf16[1024,2048]{1,0:T(8,128)(2,1)} %all-gather.8.cloned.1.call-done, f32[]{:T(128)} %bitcast), kind=kOutput, calls=%fused_computation | convolution fusion | flops 4296015872 | bytes 12582916 | tf_op jit(solution)/shard_map/dot_general | solution.py:22
  190.6 24.5 %all-gather.4.cloned.1.call-done = bf16[4096,1024]{1,0:T(8,128)(2,1)} async-done(((bf16[1024,1024]{1,0:T(8,128)(2,1)}), bf16[4096,1024]{1,0:T(8,128)(2,1)}) %all-gather.4.cloned.1.call-update) | async-done | bytes 8388624 | tf_op jit(solution)/shard_map/all_gather | solution.py:13
  215.2 10.4 %convolution_multiply_fusion.1 = f32[1024,512]{1,0:T(8,128)} fusion(bf16[4096,1024]{1,0:T(8,128)(2,1)} %all-gather.4.cloned.1.call-done, bf16[4096,512]{1,0:T(8,128)(2,1)} %all-gather.6.cloned.1.call-done, f32[]{:T(128)} %bitcast), kind=kOutput, calls=%fused_computation.1 | convolution fusion | flops 4295491584 | bytes 14680068 | tf_op jit(solution)/shard_map/dot_general | solution.py:12
Async XLA Ops:
  7.2 85.9 %all-gather.6.cloned.1.call-start = ((), (), s32[]{:S(2)}) async-start(), calls=%async_computation.2 | async-start | bytes 5242880 | tf_op jit(solution)/shard_map/all_gather | solution.py:11
  7.9 172.7 %all-gather.8.cloned.1.call-start = ((), (), s32[]{:S(2)}) async-start(), calls=%async_computation.3 | async-start | bytes 5242880 | tf_op jit(solution)/shard_map/all_gather | solution.py:21
  8.6 206.5 %all-gather.4.cloned.1.call-start = ((), (), s32[]{:S(2)}) async-start(), calls=%async_computation.1 | async-start | bytes 10485760 | tf_op jit(solution)/shard_map/all_gather | solution.py:13
  93.0 81.2 %all-to-all-start = ((bf16[4,1024,512]{2,1,0:T(8,128)(2,1)}), bf16[4,1024,512]{2,1,0:T(8,128)(2,1)}, u32[]{:S(2)}, u32[]{:S(2)}) async-start(bf16[4,1024,512]{2,1,0:T(8,128)(2,1)} %bitcast.8), calls=%async_computation | async-start | bytes 8388608 | tf_op jit(solution)/shard_map/all_to_all | solution.py:18
Sparse Core Ops, SparseCore 0:
  9.5 83.4 all-gather.5
  94.6 55.5 all-gather.7
  151.7 63.4 all-gather.3
where the time goes:
time: 232 us
  waiting for transfers between devices  186 us (80%)
  matrix products  20.4 us (9%)
  between operations  14.4 us (6%)
  local copies, waits for them, and re-layouts  6.35 us (3%)
  starting transfers between devices  4.97 us (2%)
    all_gather x1, waiting for transfers between devices, shards(): cotangent_all = lax.all_gather(expected_cot, 'markov', axis=0, tiled=True)  83.7 us
    all_to_all x1, waiting for transfers between devices, shards(): lax.all_to_all(cotangent_all, ('storage', 'sub'), split_axis=0, concat_ax...  75.7 us
    all_gather x1, waiting for transfers between devices, shards(): lax.all_gather(transition, ('storage', 'sub'), axis=0, tiled=True)  24.5 us
    dot_general x1, matrix products, shards(): lax.dot_general(lax.all_gather(transition, ('storage', 'sub'), axis=0, ti...  10.4 us
    dot_general x1, matrix products, shards(): lax.dot_general(own_states, gathered_values, (((1,), (1,)), ((), ())), pr...  10 us
    all_to_all x1, local copies, waits for them, and re-layouts, shards(): lax.all_to_all(cotangent_all, ('storage', 'sub'), split_axis=0, concat_ax...  6.35 us
    all_to_all x1, starting transfers between devices, shards(): lax.all_to_all(cotangent_all, ('storage', 'sub'), split_axis=0, concat_ax...  4.85 us
  transfers between devices with their start and end apart: 4, of which 3 were waited for; matrix products, arithmetic and copies ran while one was open for 7% of the time, Pallas kernels for 0%

commit v1 on v0

--- a/solution.py
+++ b/solution.py
@@ -8,7 +8,14 @@
 
 def shards(expected_cot, value_next, transition, section):
     discount_factor = jnp.exp(section[0].astype(jnp.float32) * jnp.log(jnp.float32(discount_rate)))
-    cotangent_all = lax.all_gather(expected_cot, "markov", axis=0, tiled=True)
+    ring = [expected_cot]
+    for hop in range(3):
+        ring.append(lax.ppermute(ring[-1], "markov", [(dev, (dev + 1) % 4) for dev in range(4)]))
+    cotangent_all = jnp.roll(
+        jnp.concatenate(ring[::-1], axis=0),
+        (lax.axis_index("markov") + 1) * ring[0].shape[0],
+        axis=0,
+    )
     adjoint_sum = lax.dot_general(
         lax.all_gather(transition, ("storage", "sub"), axis=0, tiled=True),
         cotangent_all,

time: 232 us -> 183 us (0.79)
  waiting for transfers between devices: 186 us -> 129 us
  local copies, waits for them, and re-layouts: 6.35 us -> 13.4 us
  starting transfers between devices: 4.97 us -> 8.02 us
    all_gather x1 -> x0, waiting for transfers between devices: 83.7 us -> none  [shards(): cotangent_all = lax.all_gather(expected_cot, 'markov', axis=0, tiled=True)]
    ppermute x0 -> x3, waiting for transfers between devices: none -> 76.9 us  [shards(): lax.ppermute(ring[-1], 'markov', [(dev, (dev + 1) % 4) for dev in range(4)])]
    all_to_all x1, waiting for transfers between devices: 75.7 us -> 50.3 us  [shards(): lax.all_to_all(cotangent_all, ('storage', 'sub'), split_axis=0, concat_ax...]
    all_gather x1, waiting for transfers between devices: 24.5 us -> 0.01 us  [shards(): lax.all_gather(transition, ('storage', 'sub'), axis=0, tiled=True)]
    unnamed x0 -> x10, local copies, waits for them, and re-layouts: none -> 4.84 us
    ppermute x0 -> x3, starting transfers between devices: none -> 3.11 us  [shards(): lax.ppermute(ring[-1], 'markov', [(dev, (dev + 1) % 4) for dev in range(4)])]
  transfers between devices with their start and end apart: 4 -> 6, of which waited for: 3 -> 4; matrix products, arithmetic and copies ran while one was open for 7% -> 12% of each run, Pallas kernels for 0% -> 0%
where the time goes in v1:
time: 183 us
  waiting for transfers between devices  129 us (70%)
  matrix products  18.2 us (10%)
  between operations  14.8 us (8%)
  local copies, waits for them, and re-layouts  13.4 us (7%)
  starting transfers between devices  8.02 us (4%)
    ppermute x3, waiting for transfers between devices, shards(): lax.ppermute(ring[-1], 'markov', [(dev, (dev + 1) % 4) for dev in range(4)])  76.9 us
    all_to_all x1, waiting for transfers between devices, shards(): lax.all_to_all(cotangent_all, ('storage', 'sub'), split_axis=0, concat_ax...  50.3 us
    dot_general x1, matrix products, shards(): lax.dot_general(own_states, gathered_values, (((1,), (1,)), ((), ())), pr...  10 us
    dot_general x1, matrix products, shards(): lax.dot_general(lax.all_gather(transition, ('storage', 'sub'), axis=0, ti...  8.22 us
    all_to_all x1, local copies, waits for them, and re-layouts, shards(): lax.all_to_all(cotangent_all, ('storage', 'sub'), split_axis=0, concat_ax...  6.32 us
    unnamed x10, local copies, waits for them, and re-layouts  4.84 us
    all_to_all x1, starting transfers between devices, shards(): lax.all_to_all(cotangent_all, ('storage', 'sub'), split_axis=0, concat_ax...  4.84 us
  transfers between devices with their start and end apart: 6, of which 4 were waited for; matrix products, arithmetic and copies ran while one was open for 12% of the time, Pallas kernels for 0%

profile of v1, /device:TPU:0, one launch (start us, length us, event | category | flops | bytes accessed | tf_op | source)
XLA Modules:
  0.0 183.1 jit_solution(7196318825359053925)
XLA Ops:
  7.2 0.0 all-gather.5.cloned.1.call-start
  7.2 0.7 all-gather.5.cloned.1.call-update
  7.9 0.0 all-gather.3.cloned.1.call-start
  8.0 0.7 all-gather.3.cloned.1.call-update
  8.7 3.1 %collective-permute-start = (bf16[1024,512]{1,0:T(8,128)(2,1)}, bf16[1024,512]{1,0:T(8,128)(2,1)S(1)}, u32[]{:S(2)}, u32[]{:S(2)}) collective-permute-start(bf16[1024,512]{1,0:T(8,128)(2,1)} %param.4), channel_id=1, source_target_pairs={{0,4},{4,8},{8,12},{12,0},{1,5},{5,9},{9,13},{13,1},{2,6},{6,10},{... | collective-permute-start | bytes 3145736 | tf_op jit(solution)/shard_map/ppermute | solution.py:13
  11.8 25.4 %collective-permute-done = bf16[1024,512]{1,0:T(8,128)(2,1)S(1)} collective-permute-done((bf16[1024,512]{1,0:T(8,128)(2,1)}, bf16[1024,512]{1,0:T(8,128)(2,1)S(1)}, u32[]{:S(2)}, u32[]{:S(2)}) %collective-permute-start) | collective-permute-done | bytes 1048608 | tf_op jit(solution)/shard_map/ppermute | solution.py:13
  37.2 0.0 collective-permute-start.1
  37.2 26.1 %collective-permute-done.1 = bf16[1024,512]{1,0:T(8,128)(2,1)S(1)} collective-permute-done((bf16[1024,512]{1,0:T(8,128)(2,1)S(1)}, bf16[1024,512]{1,0:T(8,128)(2,1)S(1)}, u32[]{:S(2)}, u32[]{:S(2)}) %collective-permute-start.1) | collective-permute-done | bytes 1048608 | tf_op jit(solution)/shard_map/ppermute | solution.py:13
  63.3 25.4 %collective-permute-done.2 = bf16[1024,512]{1,0:T(8,128)(2,1)} collective-permute-done((bf16[1024,512]{1,0:T(8,128)(2,1)S(1)}, bf16[1024,512]{1,0:T(8,128)(2,1)}, u32[]{:S(2)}, u32[]{:S(2)}) %collective-permute-start.2) | collective-permute-done | bytes 1048608 | tf_op jit(solution)/shard_map/ppermute | solution.py:13
  88.6 1.4 constant_dynamic-update-slice_fusion.7
  90.0 0.1 constant_dynamic-update-slice_fusion.6
  90.1 0.1 constant_dynamic-update-slice_fusion.5
  90.2 0.1 constant_dynamic-update-slice_fusion.4
  90.3 1.3 constant_dynamic-update-slice_fusion.3
  91.6 0.1 constant_dynamic-update-slice_fusion.2
  91.7 0.1 constant_dynamic-update-slice_fusion.1
  91.7 0.1 constant_dynamic-update-slice_fusion
  91.8 2.2 %constant_dynamic-slice_fusion = bf16[4096,512]{1,0:T(8,128)(2,1)} fusion(bf16[8192,512]{1,0:T(8,128)(2,1)S(1)} %constant_dynamic-update-slice_fusion, s32[]{:T(128)S(6)} %select_n.14), kind=kLoop, calls=%fused_computation.10 | loop fusion | bytes 8388612 | tf_op jit(solution)/shard_map/jit(_roll_dynamic)/dynamic_slice | solution.py:14
  94.0 4.8 %all-to-all-start = ((bf16[4,1024,512]{2,1,0:T(8,128)(2,1)}), bf16[4,1024,512]{2,1,0:T(8,128)(2,1)}, u32[]{:S(2)}, u32[]{:S(2)}) async-start(bf16[4,1024,512]{2,1,0:T(8,128)(2,1)} %bitcast.10), calls=%async_computation | async-start | bytes 8388608 | tf_op jit(solution)/shard_map/all_to_all | solution.py:25
  99.5 50.3 %all-to-all-done = bf16[4,1024,512]{2,1,0:T(8,128)(2,1)} async-done(((bf16[4,1024,512]{2,1,0:T(8,128)(2,1)}), bf16[4,1024,512]{2,1,0:T(8,128)(2,1)}, u32[]{:S(2)}, u32[]{:S(2)}) %all-to-all-start) | async-done | bytes 4194336 | tf_op jit(solution)/shard_map/all_to_all | solution.py:25
  149.9 6.3 %copy.8 = bf16[1024,4,512]{0,2,1:T(8,128)(2,1)} copy(bf16[1024,4,512]{2,0,1:T(8,128)(2,1)} %bitcast.3) | data formatting | bytes 8388608 | tf_op jit(solution)/shard_map/all_to_all | solution.py:25
  156.2 10.0 %convolution_multiply_fusion = f32[1024,1024]{1,0:T(8,128)} fusion(bf16[1024,2048]{0,1:T(8,128)(2,1)} %bitcast.11, bf16[1024,2048]{1,0:T(8,128)(2,1)} %all-gather.5.cloned.1.call-done, f32[]{:T(128)} %bitcast), kind=kOutput, calls=%fused_computation | convolution fusion | flops 4296015872 | bytes 12582916 | tf_op jit(solution)/shard_map/dot_general | solution.py:29
  166.2 8.2 %multiply_bitcast_fusion = f32[1024,512]{0,1:T(8,128)S(1)} fusion(bf16[4096,512]{1,0:T(8,128)(2,1)} %constant_dynamic-slice_fusion, bf16[4096,1024]{1,0:T(8,128)(2,1)} %all-gather.3.cloned.1.call-done, f32[]{:T(128)} %bitcast), kind=kOutput, calls=%fused_computation.1 | convolution fusion | flops 4295491584 | bytes 14680068 | tf_op jit(solution)/shard_map/dot_general | solution.py:19
  174.4 1.8 copy.9
  (5 shorter events, 0.0 us)
Async XLA Ops:
  7.2 83.0 %copy-start = (bf16[1024,512]{1,0:T(8,128)(2,1)S(1)}, bf16[1024,512]{1,0:T(8,128)(2,1)}, u32[]{:S(2)}) copy-start(bf16[1024,512]{1,0:T(8,128)(2,1)} %param.4) | copy-start | bytes 3145732
  7.2 149.0 %all-gather.5.cloned.1.call-start = ((), (), s32[]{:S(2)}) async-start(), calls=%async_computation.2 | async-start | bytes 5242880 | tf_op jit(solution)/shard_map/all_gather | solution.py:28
  7.9 158.3 %all-gather.3.cloned.1.call-start = ((), (), s32[]{:S(2)}) async-start(), calls=%async_computation.1 | async-start | bytes 10485760 | tf_op jit(solution)/shard_map/all_gather | solution.py:20
  8.7 28.5 %collective-permute-start = (bf16[1024,512]{1,0:T(8,128)(2,1)}, bf16[1024,512]{1,0:T(8,128)(2,1)S(1)}, u32[]{:S(2)}, u32[]{:S(2)}) collective-permute-start(bf16[1024,512]{1,0:T(8,128)(2,1)} %param.4), channel_id=1, source_target_pairs={{0,4},{4,8},{8,12},{12,0},{1,5},{5,9},{9,13},{13,1},{2,6},{6,10},{... | collective-permute-start | bytes 3145736 | tf_op jit(solution)/shard_map/ppermute | solution.py:13
  37.2 26.1 %collective-permute-start.1 = (bf16[1024,512]{1,0:T(8,128)(2,1)S(1)}, bf16[1024,512]{1,0:T(8,128)(2,1)S(1)}, u32[]{:S(2)}, u32[]{:S(2)}) collective-permute-start(bf16[1024,512]{1,0:T(8,128)(2,1)S(1)} %collective-permute-done), channel_id=1, source_target_pairs={{0,4},{4,8},{8,12},{12,0},{1,5},{5,9},{9,13},{13,1},{2,6},{6,10},{... | collective-permute-start | bytes 3145736 | tf_op jit(solution)/shard_map/ppermute | solution.py:13
  63.3 25.4 %collective-permute-start.2 = (bf16[1024,512]{1,0:T(8,128)(2,1)S(1)}, bf16[1024,512]{1,0:T(8,128)(2,1)}, u32[]{:S(2)}, u32[]{:S(2)}) collective-permute-start(bf16[1024,512]{1,0:T(8,128)(2,1)S(1)} %collective-permute-done.1), channel_id=1, source_target_pairs={{0,4},{4,8},{8,12},{12,0},{1,5},{5,9},{9,13},{13,1},{2,6},{6,10},{... | collective-permute-start | bytes 3145736 | tf_op jit(solution)/shard_map/ppermute | solution.py:13
  94.0 55.9 %all-to-all-start = ((bf16[4,1024,512]{2,1,0:T(8,128)(2,1)}), bf16[4,1024,512]{2,1,0:T(8,128)(2,1)}, u32[]{:S(2)}, u32[]{:S(2)}) async-start(bf16[4,1024,512]{2,1,0:T(8,128)(2,1)} %bitcast.10), calls=%async_computation | async-start | bytes 8388608 | tf_op jit(solution)/shard_map/all_to_all | solution.py:25
Sparse Core Ops, SparseCore 0:
  9.5 37.1 all-gather.4
  48.3 61.1 all-gather.2
